TPU v7x, 1024 devices: a whole 4x8x16 slice. The times are simulated.
1024 devices in a mesh: pipe: 32 (over z_hi, y, core), tensor: 8 (over z_lo), dp: 4 (over x).
Axes of the slice: x: 4, y: 8, z: 16 (z_hi: 2, z_lo: 8; z = z_hi * 8 + z_lo), core: 2. Of those that a mesh axis runs over, the one named last changes fastest.
Arguments:
- narrowing_projection_weights: bfloat16 [32, 4, 5120, 256], P('pipe', None, 'tensor'), may hold values from -0.078125 to 0.078125
- widening_projection_weights: bfloat16 [32, 4, 256, 5120], P('pipe', None, None, 'tensor'), may hold values from -0.375 to 0.375
- scaling_multipliers: float32 [32, 4, 5120], P('pipe', None, 'tensor'), may hold values from 0.5 to 1.5
- slot_entry_activation: bfloat16 [32, 4, 128, 5120], P('pipe', None, 'dp', 'tensor'), may hold values from -15 to 15
- retained_section_entries: bfloat16 [2, 32, 4, 128, 5120], P(None, 'pipe', None, 'dp', 'tensor'), may hold values from -15 to 15
- slot_result_sensitivity: bfloat16 [32, 4, 128, 5120], P('pipe', None, 'dp', 'tensor'), may hold values from -4 to 4
- fresh_micro_batches: bfloat16 [1, 2, 128, 5120], P(None, None, 'dp', 'tensor'), may hold values from -15 to 15
- latest_result_sensitivity: bfloat16 [1, 2, 128, 5120], P(None, None, 'dp', 'tensor'), may hold values from -4 to 4
Outputs:
- section_outputs: bfloat16 [32, 4, 128, 5120], P('pipe', None, 'dp', 'tensor')
- input_grads: bfloat16 [32, 4, 128, 5120], P('pipe', None, 'dp', 'tensor')
- grad_down: float32 [32, 2, 5120, 256], P('pipe', None, ('tensor', 'dp'))
- grad_up: float32 [32, 2, 256, 5120], P('pipe', None, 'dp', 'tensor')
All inputs are finite; a program needn't handle non-finite values.
Results may differ from a plain program's by a relative error of at most 0.025.
Values may be sent and summed in bfloat16 or wider, within the bound.
A program may use at most 32 MiB of HBM per device.

v0:
```python
import jax
import jax.numpy as jnp
from jax import lax
from jax.sharding import PartitionSpec as P

D = 5120


eps = 1e-06


def extended(cells, sides, width):
    for axis, dim in sides:
        count = lax.axis_size(axis)
        ends = count - 1
        head = lax.slice_in_dim(cells, 0, width, axis=dim)
        tail = lax.slice_in_dim(cells, cells.shape[dim] - width, cells.shape[dim], axis=dim)
        cells = jnp.concatenate(
            [
                lax.ppermute(tail, axis, [(i, (i + 1) % count) for i in range(ends)]),
                cells,
                lax.ppermute(head, axis, [((i + 1) % count, i) for i in range(ends)]),
            ],
            axis=dim,
        )
    return cells


def partner(value, axis, stride):
    mask = 2**stride
    pairs = [(source, source ^ mask) for source in range(lax.axis_size(axis))]
    return lax.ppermute(value, axis, pairs)


def per_device(
    narrowing_projection_weights,
    widening_projection_weights,
    scaling_multipliers,
    slot_entry_activation,
    retained_section_entries,
    slot_result_sensitivity,
    fresh_micro_batches,
    latest_result_sensitivity,
):
    holders = lax.axis_size("pipe")
    position = lax.axis_index("pipe")
    at_start = position == 0
    at_end = position == holders - 1
    w_down = narrowing_projection_weights[0]
    w_up = widening_projection_weights[0]
    gain_rows = scaling_multipliers[0]
    entry_activation_lines = slot_entry_activation[0]
    upstream = slot_result_sensitivity[0]
    grad_down = jnp.zeros(w_down.shape, jnp.float32)
    grad_up = jnp.zeros(w_up.shape, jnp.float32)
    ticks = retained_section_entries.shape[0]
    result_activation_lines = entry_activation_lines
    rows_grad = upstream
    for tick_index in range(ticks):
        stacked = jnp.stack([entry_activation_lines, retained_section_entries[tick_index, 0]])
        widened = stacked.astype(jnp.float32)
        scaled = (widened * gain_rows[None, :, None, :]).astype(jnp.bfloat16)
        part_latent = jnp.einsum(
            "csnd,sdr->csnr", scaled, w_down, preferred_element_type=jnp.float32
        )
        part_squares = jnp.sum(widened * widened, axis=-1)
        part_grad = jnp.einsum("snd,srd->snr", upstream, w_up, preferred_element_type=jnp.float32)
        latent, squares = (
            lax.psum(part_latent.astype(jnp.bfloat16), "tensor").astype(jnp.float32),
            lax.psum(part_squares.astype(jnp.bfloat16), "tensor").astype(jnp.float32),
        )
        hidden_rank_gradient = lax.psum(part_grad.astype(jnp.bfloat16), "tensor").astype(
            jnp.float32
        )
        factor = 1.0 / jnp.sqrt(squares / D + eps)
        preact = latent * factor[..., None]
        active = jax.nn.silu(preact).astype(jnp.bfloat16)
        result_activation_lines = (
            widened[0]
            + jnp.einsum("snr,srd->snd", active[0], w_up, preferred_element_type=jnp.float32)
        ).astype(jnp.bfloat16)
        sigmoid_z = jax.nn.sigmoid(preact[1])
        preact_grad = hidden_rank_gradient * sigmoid_z * (1.0 + preact[1] * (1.0 - sigmoid_z))
        latent_step = (preact_grad * factor[1][..., None]).astype(jnp.bfloat16)
        gradient_squares = -0.5 * factor[1] ** 3 / D * jnp.sum(preact_grad * latent[1], axis=-1)
        feature_grad = (
            jnp.einsum("snr,sdr->snd", latent_step, w_down, preferred_element_type=jnp.float32)
            * gain_rows[:, None, :]
        )
        rows_grad = (
            feature_grad
            + 2.0 * widened[1] * gradient_squares[..., None]
            + upstream.astype(jnp.float32)
        ).astype(jnp.bfloat16)
        grad_down = grad_down + jnp.einsum(
            "snd,snr->sdr", scaled[1], latent_step, preferred_element_type=jnp.float32
        )
        grad_up = grad_up + jnp.einsum(
            "snr,snd->srd", active[1], upstream, preferred_element_type=jnp.float32
        )
        if tick_index + 1 < ticks:
            to_lower = jnp.stack(
                [result_activation_lines[1], result_activation_lines[2], rows_grad[0], rows_grad[3]]
            )
            to_upper = jnp.stack(
                [result_activation_lines[0], result_activation_lines[3], rows_grad[1], rows_grad[2]]
            )
            padded = extended(jnp.stack([to_lower, to_upper]), (("pipe", 0),), 1)
            from_below = padded[0]
            from_above = padded[3]
            entering = fresh_micro_batches[tick_index]
            arriving = latest_result_sensitivity[tick_index]
            entry_activation_lines = jnp.stack(
                [
                    jnp.where(at_start, entering[0], from_below[0]),
                    jnp.where(at_end, result_activation_lines[0], from_above[0]),
                    jnp.where(at_end, entering[1], from_above[1]),
                    jnp.where(at_start, result_activation_lines[2], from_below[1]),
                ]
            )
            upstream = jnp.stack(
                [
                    jnp.where(at_end, rows_grad[1], from_above[2]),
                    jnp.where(at_start, arriving[0], from_below[2]),
                    jnp.where(at_start, rows_grad[3], from_below[3]),
                    jnp.where(at_end, arriving[1], from_above[3]),
                ]
            )
    summed_down, summed_up = (
        lax.psum_scatter(
            grad_down.astype(jnp.bfloat16), "dp", scatter_dimension=1, tiled=True
        ).astype(jnp.float32),
        lax.psum_scatter(
            grad_up.astype(jnp.bfloat16), "dp", scatter_dimension=1, tiled=True
        ).astype(jnp.float32),
    )
    far_down = summed_down[2:]
    far_up = summed_up[2:]
    count_down = far_down.size
    flattened = jnp.concatenate([far_down.reshape(-1), far_up.reshape(-1)])
    for bit_index in range(holders.bit_length() - 1):
        flattened = partner(flattened.astype(jnp.bfloat16), "pipe", bit_index).astype(
            flattened.dtype
        )
    mirrored_down = flattened[:count_down].reshape(far_down.shape)
    mirrored_up = flattened[count_down:].reshape(far_up.shape)
    total_down = summed_down[:2] + mirrored_down
    total_up = summed_up[:2] + mirrored_up
    return (result_activation_lines[None], rows_grad[None], total_down[None], total_up[None])


def solution(mesh):
    return jax.shard_map(
        per_device,
        mesh=mesh,
        in_specs=(
            P("pipe", None, "tensor", None),
            P("pipe", None, None, "tensor"),
            P("pipe", None, "tensor"),
            P("pipe", None, "dp", "tensor"),
            P(None, "pipe", None, "dp", "tensor"),
            P("pipe", None, "dp", "tensor"),
            P(None, None, "dp", "tensor"),
            P(None, None, "dp", "tensor"),
        ),
        out_specs=(
            P("pipe", None, "dp", "tensor"),
            P("pipe", None, "dp", "tensor"),
            P("pipe", None, ("tensor", "dp"), None),
            P("pipe", None, "dp", "tensor"),
        ),
        check_vma=False,
    )
```

profile of v0, /device:TPU:88, one launch (start us, length us, event | category | flops | bytes accessed | tf_op | source)
XLA Modules:
  0.0 504.9 jit_solution(10205981697480209019)
XLA Ops:
  7.2 1.8 slice_bitcast_fusion.9
  9.0 2.5 fusion.70
  13.6 1.1 maximum_convert_fusion
  14.6 30.5 %psum.43 = bf16[2,4,32]{2,1,0:T(4,128)(2,1)S(1)} all-reduce(bf16[2,4,32]{2,1,0:T(4,128)(2,1)S(1)} %get-tuple-element.14), channel_id=1, replica_groups=mesh['pipe'=32,'tensor'=8,'dp'=4] {'tensor'}, use_global_device_ids=true, to_apply=%region_2.0 | all-reduce | flops 256 | bytes 1024 | tf_op jit(solution)/shard_map/psum | solution.py:70
  45.1 97.1 %all-reduce.7.cloned.1.call-done = (bf16[2,4,32,256]{3,2,0,1:T(8,128)(2,1)}, bf16[4,32,256]{2,1,0:T(8,128)(2,1)}) async-done(((bf16[2,4,32,256]{3,2,0,1:T(8,128)(2,1)}, bf16[4,32,256]{2,1,0:T(8,128)(2,1)}), (bf16[2,4,32,256]{3,2,0,1:T(8,128)(2,1)}, bf16[4,32,256]{2,1,0:T(8,128)(2,1)})) %all-reduce.7.cloned.1.call-update) | async-done | bytes 196624 | tf_op jit(solution)/shard_map/psum | solution.py:69
  143.2 1.1 multiply_convert_fusion.3
  145.8 1.9 collective-permute-start.1
  147.8 2.5 collective-permute-start
  150.3 2.1 fusion.79
  152.4 2.1 collective-permute-done
  155.5 32.6 %psum.46 = bf16[2,4,32]{2,1,0:T(4,128)(2,1)S(1)} all-reduce(bf16[2,4,32]{2,1,0:T(4,128)(2,1)S(1)} %get-tuple-element.13), channel_id=1, replica_groups=mesh['pipe'=32,'tensor'=8,'dp'=4] {'tensor'}, use_global_device_ids=true, to_apply=%region_7.8 | all-reduce | flops 256 | bytes 1024 | tf_op jit(solution)/shard_map/psum | solution.py:70
  188.1 1.0 fusion.67
  189.1 1.1 fusion.73
  190.3 128.4 %all-reduce.5.cloned.1.call-done = (bf16[2,4,32,256]{3,2,1,0:T(8,128)(2,1)}, bf16[4,32,256]{2,1,0:T(8,128)(2,1)}) async-done(((bf16[2,4,32,256]{3,2,1,0:T(8,128)(2,1)}, bf16[4,32,256]{2,1,0:T(8,128)(2,1)}), (bf16[2,4,32,256]{3,2,1,0:T(8,128)(2,1)}, bf16[4,32,256]{2,1,0:T(8,128)(2,1)})) %all-reduce.5.cloned.1.call-update) | async-done | bytes 196624 | tf_op jit(solution)/shard_map/psum | solution.py:69
  318.7 1.7 broadcast_multiply_fusion
  321.1 3.4 add_convert_fusion.1
  326.3 1.6 add_convert_fusion
  327.9 33.2 %reduce-scatter.3.cloned.1.call-done = bf16[4,160,256]{2,1,0:T(8,128)(2,1)} async-done(((bf16[4,640,256]{2,1,0:T(8,128)(2,1)}), bf16[4,160,256]{2,1,0:T(8,128)(2,1)}) %reduce-scatter.3.cloned.1.call-update) | async-done | bytes 327696 | tf_op jit(solution)/shard_map/reduce_scatter | solution.py:130
  362.2 37.5 %reduce-scatter.5.cloned.1.call-done = bf16[4,64,640]{2,1,0:T(8,128)(2,1)} async-done(((bf16[4,256,640]{2,1,0:T(8,128)(2,1)}), bf16[4,64,640]{2,1,0:T(8,128)(2,1)}) %reduce-scatter.5.cloned.1.call-update) | async-done | bytes 327696 | tf_op jit(solution)/shard_map/reduce_scatter | solution.py:133
  399.7 1.6 slice.264
  401.3 1.7 reshape.171
  404.0 1.9 collective-permute-start.2
  405.9 1.6 collective-permute-done.2
  407.5 2.5 collective-permute-start.3
  410.0 9.2 %collective-permute-done.3 = bf16[163840]{0:T(1024)(128)(2,1)S(1)} collective-permute-done((bf16[163840]{0:T(1024)(128)(2,1)S(1)}, bf16[163840]{0:T(1024)(128)(2,1)S(1)}, u32[]{:S(2)}, u32[]{:S(2)}) %collective-permute-start.3) | collective-permute-done | bytes 327712 | tf_op jit(solution)/shard_map/ppermute | solution.py:32
  419.1 2.4 collective-permute-start.4
  422.6 15.3 %collective-permute-done.4 = bf16[163840]{0:T(1024)(128)(2,1)S(1)} collective-permute-done((bf16[163840]{0:T(1024)(128)(2,1)S(1)}, bf16[163840]{0:T(1024)(128)(2,1)S(1)}, u32[]{:S(2)}, u32[]{:S(2)}) %collective-permute-start.4) | collective-permute-done | bytes 327712 | tf_op jit(solution)/shard_map/ppermute | solution.py:32
  437.8 4.7 collective-permute-start.5
  442.7 16.0 %collective-permute-done.5 = bf16[163840]{0:T(1024)(128)(2,1)S(1)} collective-permute-done((bf16[163840]{0:T(1024)(128)(2,1)S(1)}, bf16[163840]{0:T(1024)(128)(2,1)S(1)}, u32[]{:S(2)}, u32[]{:S(2)}) %collective-permute-start.5) | collective-permute-done | bytes 327712 | tf_op jit(solution)/shard_map/ppermute | solution.py:32
  458.7 12.5 %collective-permute-start.6 = (bf16[163840]{0:T(1024)(128)(2,1)S(1)}, bf16[163840]{0:T(1024)(128)(2,1)S(1)}, u32[]{:S(2)}, u32[]{:S(2)}) collective-permute-start(bf16[163840]{0:T(1024)(128)(2,1)S(1)} %collective-permute-done.5), channel_id=1, source_target_pairs={{0,512},{32,544},{64,576},{96,608},{128,640},{160,672},{192,704},{... | collective-permute-start | bytes 983048 | tf_op jit(solution)/shard_map/ppermute | solution.py:32
  472.3 1.2 fusion.58
  473.4 23.1 %collective-permute-done.6 = bf16[163840]{0:T(1024)(128)(2,1)S(1)} collective-permute-done((bf16[163840]{0:T(1024)(128)(2,1)S(1)}, bf16[163840]{0:T(1024)(128)(2,1)S(1)}, u32[]{:S(2)}, u32[]{:S(2)}) %collective-permute-start.6) | collective-permute-done | bytes 327712 | tf_op jit(solution)/shard_map/ppermute | solution.py:32
  (94 shorter events, 13.7 us)
Async XLA Ops:
  7.2 5.3 %copy-start = (bf16[1,4,640,256]{3,2,1,0:T(8,128)(2,1)S(1)}, bf16[1,4,640,256]{3,2,1,0:T(8,128)(2,1)}, u32[]{:S(2)}) copy-start(bf16[1,4,640,256]{3,2,1,0:T(8,128)(2,1)} %param.8) | copy-start | bytes 3932164
  7.2 4.4 copy-start.8
  7.2 4.4 copy-start.22
  7.2 135.0 %all-reduce.7.cloned.1.call-start = ((), (), s32[]{:S(2)}) async-start(), calls=%async_computation.5 | async-start | bytes 393216 | tf_op jit(solution)/shard_map/psum | solution.py:69
  13.5 130.8 %copy-start.1 = (bf16[1,4,256,640]{3,2,1,0:T(8,128)(2,1)S(1)}, bf16[1,4,256,640]{3,2,1,0:T(8,128)(2,1)}, u32[]{:S(2)}) copy-start(bf16[1,4,256,640]{3,2,1,0:T(8,128)(2,1)} %param.9) | copy-start | bytes 3932164
  13.5 305.2 %all-reduce.5.cloned.1.call-start = ((), (), s32[]{:S(2)}) async-start(), calls=%async_computation.4 | async-start | bytes 393216 | tf_op jit(solution)/shard_map/psum | solution.py:69
  143.2 1.5 copy-start.9
  144.3 1.0 copy-start.4
  145.2 5.1 %copy-start.3 = (bf16[2,4,32,640]{3,2,1,0:T(8,128)(2,1)S(1)}, bf16[2,4,32,640]{3,2,1,0:T(8,128)(2,1)}, u32[]{:S(2)}) copy-start(bf16[2,4,32,640]{3,2,1,0:T(8,128)(2,1)} %copy-done.2) | copy-start | bytes 983044
  145.8 6.6 %collective-permute-start.1 = (bf16[1,4,32,640]{3,2,1,0:T(8,128)(2,1)S(1)}, bf16[1,4,32,640]{3,2,1,0:T(8,128)(2,1)S(1)}, u32[]{:S(2)}, u32[]{:S(2)}) collective-permute-start(bf16[1,4,32,640]{3,2,1,0:T(8,128)(2,1)S(1)} %maximum_bitcast_fusion.1), channel_id=1, source_target_pairs={{32,0},{64,32},{96,64},{128,96},{160,128},{192,160},{224,192},{256... | collective-permute-start | bytes 491528 | tf_op jit(solution)/shard_map/ppermute | solution.py:22
  147.8 6.8 %copy-start.23 = (bf16[1,2,32,640]{3,2,1,0:T(8,128)(2,1)S(1)}, bf16[1,2,32,640]{3,2,1,0:T(8,128)(2,1)}, u32[]{:S(2)}) copy-start(bf16[1,2,32,640]{3,2,1,0:T(8,128)(2,1)} %param.15) | copy-start | bytes 245764
  147.8 6.8 %copy-start.24 = (bf16[1,2,32,640]{3,2,1,0:T(8,128)(2,1)S(1)}, bf16[1,2,32,640]{3,2,1,0:T(8,128)(2,1)}, u32[]{:S(2)}) copy-start(bf16[1,2,32,640]{3,2,1,0:T(8,128)(2,1)} %param.14) | copy-start | bytes 245764
  147.8 6.8 %collective-permute-start = (bf16[1,4,32,640]{3,2,1,0:T(8,128)(2,1)S(1)}, bf16[1,4,32,640]{3,2,1,0:T(8,128)(2,1)S(1)}, u32[]{:S(2)}, u32[]{:S(2)}) collective-permute-start(bf16[1,4,32,640]{3,2,1,0:T(8,128)(2,1)S(1)} %maximum_bitcast_fusion), channel_id=1, source_target_pairs={{0,32},{32,64},{64,96},{96,128},{128,160},{160,192},{192,224},{224... | collective-permute-start | bytes 491528 | tf_op jit(solution)/shard_map/ppermute | solution.py:20
  152.4 2.9 copy-start.5
  188.1 1.0 copy-start.14
  188.1 1.0 copy-start.16
  190.3 170.9 %reduce-scatter.3.cloned.1.call-start = ((), (), s32[]{:S(2)}) async-start(), calls=%async_computation.2 | async-start | bytes 1638400 | tf_op jit(solution)/shard_map/reduce_scatter | solution.py:130
  324.6 0.9 copy-start.13
  324.6 1.4 copy-start.10
  324.6 1.4 copy-start.15
  324.6 75.0 %reduce-scatter.5.cloned.1.call-start = ((), (), s32[]{:S(2)}) async-start(), calls=%async_computation.3 | async-start | bytes 1638400 | tf_op jit(solution)/shard_map/reduce_scatter | solution.py:133
  362.2 80.3 %copy-start.7 = (f32[2,4,32,256]{3,2,1,0:T(8,128)S(1)}, f32[2,4,32,256]{3,2,1,0:T(8,128)}, u32[]{:S(2)}) copy-start(f32[2,4,32,256]{3,2,1,0:T(8,128)} %copy-done.6) | copy-start | bytes 786436
  403.0 39.6 %copy-start.21 = (bf16[4,32,256]{2,1,0:T(8,128)(2,1)S(1)}, bf16[4,32,256]{2,1,0:T(8,128)(2,1)}, u32[]{:S(2)}) copy-start(bf16[4,32,256]{2,1,0:T(8,128)(2,1)} %get-tuple-element.5) | copy-start | bytes 196612
  403.0 68.3 %copy-start.11 = (bf16[2,4,32,256]{3,2,1,0:T(8,128)(2,1)S(1)}, bf16[2,4,32,256]{3,2,1,0:T(8,128)(2,1)}, u32[]{:S(2)}) copy-start(bf16[2,4,32,256]{3,2,1,0:T(8,128)(2,1)} %get-tuple-element.33) | copy-start | bytes 393220
  404.0 3.5 collective-permute-start.2
  407.5 11.6 %collective-permute-start.3 = (bf16[163840]{0:T(1024)(128)(2,1)S(1)}, bf16[163840]{0:T(1024)(128)(2,1)S(1)}, u32[]{:S(2)}, u32[]{:S(2)}) collective-permute-start(bf16[163840]{0:T(1024)(128)(2,1)S(1)} %collective-permute-done.2), channel_id=1, source_target_pairs={{0,64},{32,96},{64,0},{96,32},{128,192},{160,224},{192,128},{224,1... | collective-permute-start | bytes 983048 | tf_op jit(solution)/shard_map/ppermute | solution.py:32
  419.1 18.7 %collective-permute-start.4 = (bf16[163840]{0:T(1024)(128)(2,1)S(1)}, bf16[163840]{0:T(1024)(128)(2,1)S(1)}, u32[]{:S(2)}, u32[]{:S(2)}) collective-permute-start(bf16[163840]{0:T(1024)(128)(2,1)S(1)} %collective-permute-done.3), channel_id=1, source_target_pairs={{0,128},{32,160},{64,192},{96,224},{128,0},{160,32},{192,64},{224,... | collective-permute-start | bytes 983048 | tf_op jit(solution)/shard_map/ppermute | solution.py:32
  421.6 50.7 %copy-start.18 = (bf16[1,32,640]{2,1,0:T(8,128)(2,1)S(1)}, bf16[1,32,640]{2,1,0:T(8,128)(2,1)}, u32[]{:S(2)}) copy-start(bf16[1,32,640]{2,1,0:T(8,128)(2,1)} %get-tuple-element.27) | copy-start | bytes 122884
  437.8 20.9 %collective-permute-start.5 = (bf16[163840]{0:T(1024)(128)(2,1)S(1)}, bf16[163840]{0:T(1024)(128)(2,1)S(1)}, u32[]{:S(2)}, u32[]{:S(2)}) collective-permute-start(bf16[163840]{0:T(1024)(128)(2,1)S(1)} %collective-permute-done.4), channel_id=1, source_target_pairs={{0,256},{32,288},{64,320},{96,352},{128,384},{160,416},{192,448},{... | collective-permute-start | bytes 983048 | tf_op jit(solution)/shard_map/ppermute | solution.py:32
  458.7 37.8 %collective-permute-start.6 = (bf16[163840]{0:T(1024)(128)(2,1)S(1)}, bf16[163840]{0:T(1024)(128)(2,1)S(1)}, u32[]{:S(2)}, u32[]{:S(2)}) collective-permute-start(bf16[163840]{0:T(1024)(128)(2,1)S(1)} %collective-permute-done.5), channel_id=1, source_target_pairs={{0,512},{32,544},{64,576},{96,608},{128,640},{160,672},{192,704},{... | collective-permute-start | bytes 983048 | tf_op jit(solution)/shard_map/ppermute | solution.py:32
  473.4 23.4 %copy-start.20 = (bf16[4,64,640]{2,1,0:T(8,128)(2,1)S(1)}, bf16[4,64,640]{2,1,0:T(8,128)(2,1)}, u32[]{:S(2)}) copy-start(bf16[4,64,640]{2,1,0:T(8,128)(2,1)} %reduce-scatter.5.cloned.1.call-done) | copy-start | bytes 983044
  496.6 1.0 copy-start.19
  (4 other events, 2.9 us)
Sparse Core Ops, SparseCore 0:
  13.7 128.5 all-reduce.6
  190.4 128.3 all-reduce.4
  324.7 36.3 reduce-scatter.2
  364.4 35.2 reduce-scatter.4
where the time goes:
time: 506 us; the launch traced here: 505 us
  waiting for transfers between devices  364 us (72%)
  blocking collectives  63 us (12%)
  starting transfers between devices  28.7 us (6%)
  matrix products  16.3 us (3%)
  between operations  14.2 us (3%)
  other arithmetic  9.68 us (2%)
  local copies, waits for them, and re-layouts  9.41 us (2%)
    psum x2, waiting for transfers between devices, per_device(): lax.psum(part_latent.astype(jnp.bfloat16), 'tensor').astype(jnp.float32)  226 us
    ppermute x5, waiting for transfers between devices, partner(): return lax.ppermute(value, axis, pairs)  65.2 us
    psum x2, blocking collectives, per_device(): lax.psum(part_squares.astype(jnp.bfloat16), 'tensor').astype(jnp.float32)  63 us
    reduce_scatter x1, waiting for transfers between devices, per_device(): lax.psum_scatter(grad_up.astype(jnp.bfloat16), 'dp', scatter_dimension=1,...  37.5 us
    reduce_scatter x1, waiting for transfers between devices, per_device(): lax.psum_scatter(grad_down.astype(jnp.bfloat16), 'dp', scatter_dimension=...  33.2 us
    ppermute x5, starting transfers between devices, partner(): return lax.ppermute(value, axis, pairs)  24 us
  transfers between devices with their start and end apart: 11, of which 10 were waited for; matrix products, arithmetic and copies ran while one was open for 2% of the time, Pallas kernels for 0%

commit v1 on v0

v1 whole, which is shorter than its diff:
```python
import functools

import jax
import jax.numpy as jnp
from jax import lax
from jax.experimental import pallas as pl
from jax.experimental.pallas import tpu as pltpu
from jax.sharding import PartitionSpec as P

MESH = pl.DeviceIdType.MESH
EPS = 1e-06
F32 = jnp.float32
BF16 = jnp.bfloat16

RS1, RS1B, AG1, AG1B, RS2, AG2 = 0, 8, 16, 24, 32, 40
UP, DOWN = 48, 52
XHG, XDY0, XDY1, XA, XDU0, XDU1 = 56, 60, 64, 68, 76, 80
MIRROR = 84
N_SEMS = 86


def nt(a, b):
    return lax.dot_general(a, b, (((1,), (1,)), ((), ())), preferred_element_type=F32)


def tn(a, b):
    return lax.dot_general(a, b, (((0,), (0,)), ((), ())), preferred_element_type=F32)


def nn(a, b):
    return jnp.dot(a, b, preferred_element_type=F32)


def lanes_of(rows, *columns):
    lane = lax.broadcasted_iota(jnp.int32, (rows, 128), 1)
    out = jnp.zeros((rows, 128), F32)
    for i, column in enumerate(columns):
        out = jnp.where(lane == i, column, out)
    return out.astype(BF16)


def kernel(
    n_pipe, n_tensor, n_dp, d_model,
    wd_hbm, wu_hbm, g_hbm, x_hbm, h_hbm, dy_hbm, fresh_hbm, latest_hbm,
    y_out, dh_out, gd_out, gu_out,
    wd, wu, g, x0, h, dy0, fresh, latest,
    hg, s1, r1, s1b, r1b, a1, a1b, s2, r2, a2, ys, ds, x1, dy1,
    hgr, dyr, ar, dur, gd, gu, msd, msu, mrd, mru, y1, dh1, god, gou,
    in_sem, own_sem, out_sem, send_sem, recv_sem,
):
    p = lax.axis_index("pipe")
    t = lax.axis_index("tensor")
    k = lax.axis_index("dp")
    last = n_pipe - 1
    slots, rows, width = x0.shape
    rank = wd.shape[2]
    half = rows // 2
    not_first, not_last = p > 0, p < last
    mirror = last - p

    barrier = pltpu.get_barrier_semaphore()

    def greet(**where):
        pl.semaphore_signal(barrier, inc=1, device_id=where, device_id_type=MESH)

    greet(pipe=mirror)
    for j in range(1, n_tensor):
        greet(tensor=lax.rem(t + j, n_tensor))

    @pl.when(not_first)
    def _():
        greet(pipe=p - 1)

    @pl.when(not_last)
    def _():
        greet(pipe=p + 1)

    for j in range(1, n_dp):
        greet(dp=lax.rem(k + j, n_dp))

    loads = {}
    for i, (name, src, dst) in enumerate([
        ("x", x_hbm.at[0], x0), ("h0", h_hbm.at[0, 0], h.at[0]), ("h1", h_hbm.at[1, 0], h.at[1]),
        ("g", g_hbm.at[0], g), ("wd", wd_hbm.at[0], wd), ("dy", dy_hbm.at[0], dy0),
        ("wu", wu_hbm.at[0], wu), ("fresh", fresh_hbm.at[0], fresh), ("latest", latest_hbm.at[0], latest),
    ]):
        loads[name] = pltpu.make_async_copy(src, dst, in_sem.at[i])
        loads[name].start()

    pending = []

    def send(src, dst, index, **where):
        copy = pltpu.make_async_remote_copy(
            src_ref=src, dst_ref=dst, send_sem=send_sem.at[index], recv_sem=recv_sem.at[index],
            device_id=where, device_id_type=MESH,
        )
        copy.start()
        return copy

    def to_peers(base, axis, src_of, dst, steps):
        me, count = {"tensor": (t, n_tensor), "dp": (k, n_dp)}[axis]
        copies = []
        for j in steps:
            peer = lax.rem(me + j, count)
            copies.append(send(src_of(peer), dst, base + j, **{axis: peer}))
        pending.extend(copies)
        return copies

    ring = [4, 3, 5, 2, 6, 1, 7] if n_tensor == 8 else list(range(1, n_tensor))
    near = list(range(1, n_dp))

    for name in ("x", "h0", "h1", "g", "wd", "dy", "wu"):
        loads[name].wait()
    for s in range(slots):
        gain = g[s : s + 1, :]
        xf, h0f, h1f = x0[s].astype(F32), h[0, s].astype(F32), h[1, s].astype(F32)
        h0s, h1s = (h0f * gain).astype(BF16), (h1f * gain).astype(BF16)
        hg[s, 0:rows] = h0s
        hg[s, rows : 2 * rows] = h1s
        stacked = jnp.concatenate([(xf * gain).astype(BF16), h0s, h1s], axis=0)
        part = nn(stacked, wd[s]).astype(BF16)
        grad = nt(dy0[s], wu[s]).astype(BF16)
        sums = [jnp.sum(v * v, axis=1, keepdims=True) for v in (xf, h0f, h1f)]
        squares = lanes_of(rows, *sums)
        for i in range(2):
            lo, hi = i * half, (i + 1) * half
            r = 2 * s + i
            s1[r, :, 0:rank] = part[lo:hi]
            s1[r, :, rank : 2 * rank] = part[rows + lo : rows + hi]
            s1[r, :, 2 * rank : 3 * rank] = grad[lo:hi]
            s1[r, :, 3 * rank : 3 * rank + 128] = squares[lo:hi]
            s1b[r] = part[2 * rows + lo : 2 * rows + hi]

    pl.semaphore_wait(barrier, n_tensor - 1 + n_dp - 1 + 1 + not_first.astype(jnp.int32) + not_last.astype(jnp.int32))

    rs1 = to_peers(RS1, "tensor", lambda peer: s1.at[peer], r1.at[t], ring)
    rs1b = to_peers(RS1B, "tensor", lambda peer: s1b.at[peer], r1b.at[t], ring)

    def window(peer):
        return hg.at[:, :, pl.ds(pl.multiple_of(peer * 128, 128), 256)]

    xhg = to_peers(XHG, "dp", window, hgr.at[k], near)
    xdy0 = to_peers(XDY0, "dp", lambda peer: dy0, dyr.at[k, 0], near)
    own_hg = pltpu.make_async_copy(window(k), hgr.at[k], own_sem.at[0])
    own_hg.start()
    dyr[k, 0] = dy0[...]

    total = s1[t].astype(F32)
    for i, copy in enumerate(rs1):
        copy.wait_recv()
        total = total + r1[lax.rem(t + n_tensor - ring[i], n_tensor)].astype(F32)

    def factor_of(column):
        return 1.0 / jnp.sqrt(column / d_model + EPS)

    fx = factor_of(total[:, 3 * rank : 3 * rank + 1])
    f0 = factor_of(total[:, 3 * rank + 1 : 3 * rank + 2])
    f1 = factor_of(total[:, 3 * rank + 2 : 3 * rank + 3])

    def back(latent, factor, da):
        z = latent * factor
        sig = jax.nn.sigmoid(z)
        dz = da * sig * (1.0 + z * (1.0 - sig))
        dss = -0.5 * factor * factor * factor / d_model * jnp.sum(dz * latent, axis=1, keepdims=True)
        high = dss.astype(BF16).astype(F32)
        return (z * sig).astype(BF16), (dz * factor).astype(BF16), lanes_of(half, high, dss - high)

    def swish(z):
        return (z * jax.nn.sigmoid(z)).astype(BF16)

    ah0, du0, dss0 = back(total[:, rank : 2 * rank], f0, total[:, 2 * rank : 3 * rank])
    a1[t, :, 0:rank] = swish(total[:, 0:rank] * fx)
    a1[t, :, rank : 2 * rank] = du0
    a1[t, :, 2 * rank : 2 * rank + 128] = dss0
    ag1 = to_peers(AG1, "tensor", lambda peer: a1.at[t], a1.at[t], ring)
    u1 = s1b[t].astype(F32)
    for i, copy in enumerate(rs1b):
        copy.wait_recv()
        u1 = u1 + r1b[lax.rem(t + n_tensor - ring[i], n_tensor)].astype(F32)
    a1b[t, :, 0:rank] = ah0
    a1b[t, :, rank : 2 * rank] = swish(u1 * f1)
    ag1b = to_peers(AG1B, "tensor", lambda peer: a1b.at[t], a1b.at[t], ring)

    def gathered(ref, s, lo, hi):
        return jnp.concatenate([ref[2 * s, :, lo:hi], ref[2 * s + 1, :, lo:hi]], axis=0)

    def outputs(ref, s, rows_in, kept, cot):
        act = gathered(ref, s, 0, rank)
        du = gathered(ref, s, rank, 2 * rank)
        pair = gathered(ref, s, 2 * rank, 2 * rank + 128).astype(F32)
        dss = pair[:, 0:1] + pair[:, 1:2]
        y = (rows_in.astype(F32) + nn(act, wu[s])).astype(BF16)
        feature = nt(du, wd[s]) * g[s : s + 1, :]
        dh = (feature + 2.0 * kept.astype(F32) * dss + cot.astype(F32)).astype(BF16)
        return y, dh

    loads["fresh"].wait()
    loads["latest"].wait()

    @pl.when(jnp.logical_not(not_first))
    def _():
        x1[0] = fresh[0]
        dy1[1] = latest[0]

    @pl.when(jnp.logical_not(not_last))
    def _():
        x1[2] = fresh[1]
        dy1[3] = latest[1]

    for copy in ag1:
        copy.wait_recv()

    def upward(s, up):
        src, dst = (ys, x1) if up else (ds, dy1)
        return src.at[s], dst.at[s]

    y_up = [True, False, False, True]
    up_index = {("y", 0): 0, ("y", 3): 1, ("d", 1): 2, ("d", 2): 3}
    down_index = {("y", 1): 0, ("y", 2): 1, ("d", 0): 2, ("d", 3): 3}

    def shift(kind, s):
        src, dst = (ys.at[s], x1.at[s]) if kind == "y" else (ds.at[s], dy1.at[s])
        if (kind, s) in up_index:
            return not_last, not_first, UP + up_index[kind, s], p + 1, src, dst
        return not_first, not_last, DOWN + down_index[kind, s], p - 1, src, dst

    def shift_copy(kind, s):
        can_send, can_receive, index, peer, src, dst = shift(kind, s)
        return can_send, can_receive, pltpu.make_async_remote_copy(
            src_ref=src, dst_ref=dst, send_sem=send_sem.at[index], recv_sem=recv_sem.at[index],
            device_id={"pipe": peer}, device_id_type=MESH,
        )

    def start_shift(kind, s):
        can_send, _, copy = shift_copy(kind, s)

        @pl.when(can_send)
        def _():
            copy.start()

    def land(kind, s):
        _, can_receive, copy = shift_copy(kind, s)

        @pl.when(can_receive)
        def _():
            copy.wait_recv()

    def drain(kind, s):
        can_send, _, copy = shift_copy(kind, s)

        @pl.when(can_send)
        def _():
            copy.wait_send()

    for s in range(slots):
        y, dh = outputs(a1, s, x0[s], h[0, s], dy0[s])
        ys[s] = y
        ds[s] = dh
        start_shift("y", s)
        start_shift("d", s)

    @pl.when(jnp.logical_not(not_first))
    def _():
        x1[3] = ys[2]
        dy1[2] = ds[3]

    @pl.when(jnp.logical_not(not_last))
    def _():
        x1[1] = ys[0]
        dy1[0] = ds[1]

    xdu0 = to_peers(XDU0, "dp", lambda peer: a1.at[:, :, rank : 2 * rank], dur.at[k, 0], near)
    dur[k, 0] = a1[:, :, rank : 2 * rank]
    for copy in ag1b:
        copy.wait_recv()

    def latents(peer, tick):
        start = pl.multiple_of(tick * rank + peer // 2 * 128, 128)
        return a1b.at[:, :, pl.ds(start, 128)]

    xa = [
        to_peers(XA + 4 * tick, "dp", functools.partial(latents, tick=tick), ar.at[k, tick], near)
        for tick in range(2)
    ]
    own_a = [pltpu.make_async_copy(latents(k, tick), ar.at[k, tick], own_sem.at[1 + tick]) for tick in range(2)]
    for copy in own_a:
        copy.start()

    for s in range(slots):
        land("y", s)
        land("d", s)
        gain = g[s : s + 1, :]
        xf = x1[s].astype(F32)
        part = nn((xf * gain).astype(BF16), wd[s]).astype(BF16)
        grad = nt(dy1[s], wu[s]).astype(BF16)
        squares = lanes_of(rows, jnp.sum(xf * xf, axis=1, keepdims=True))
        for i in range(2):
            lo, hi = i * half, (i + 1) * half
            r = 2 * s + i
            s2[r, :, 0:rank] = part[lo:hi]
            s2[r, :, rank : 2 * rank] = grad[lo:hi]
            s2[r, :, 2 * rank : 2 * rank + 128] = squares[lo:hi]
    rs2 = to_peers(RS2, "tensor", lambda peer: s2.at[peer], r2.at[t], ring)
    xdy1 = to_peers(XDY1, "dp", lambda peer: dy1, dyr.at[k, 1], near)
    dyr[k, 1] = dy1[...]

    total = s2[t].astype(F32)
    for i, copy in enumerate(rs2):
        copy.wait_recv()
        total = total + r2[lax.rem(t + n_tensor - ring[i], n_tensor)].astype(F32)
    fx = factor_of(total[:, 2 * rank : 2 * rank + 1])
    _, du1, dss1 = back(u1, f1, total[:, rank : 2 * rank])
    a2[t, :, 0:rank] = swish(total[:, 0:rank] * fx)
    a2[t, :, rank : 2 * rank] = du1
    a2[t, :, 2 * rank : 2 * rank + 128] = dss1
    ag2 = to_peers(AG2, "tensor", lambda peer: a2.at[t], a2.at[t], ring)

    for copy in own_a:
        copy.wait()
    for copy in xdy0 + xdy1 + xa[0] + xa[1]:
        copy.wait_recv()

    def all_rows(ref, s):
        return jnp.concatenate(
            [ref[q, tick, 2 * s + i] for q in range(n_dp) for tick in range(2) for i in range(2)], axis=0
        )

    def up_gradient(s):
        cot = jnp.concatenate([dyr[q, tick, s] for q in range(n_dp) for tick in range(2)], axis=0)
        return tn(all_rows(ar, s), cot)

    keep_up = pl.ds(pl.multiple_of(lax.rem(k, 2) * 64, 64), 64)
    for s in (2, 3, 0, 1):
        gu[s] = up_gradient(s)
        if s >= 2:
            msu[s - 2] = gu[s, keep_up, :].astype(BF16)
        if s == 3:
            mu = send(msu, mru, MIRROR, pipe=mirror)

    for copy in ag2:
        copy.wait_recv()
    xdu1 = to_peers(XDU1, "dp", lambda peer: a2.at[:, :, rank : 2 * rank], dur.at[k, 1], near)
    dur[k, 1] = a2[:, :, rank : 2 * rank]

    for s in range(slots):
        y, dh = outputs(a2, s, x1[s], h[1, s], dy1[s])
        y1[s] = y
        dh1[s] = dh
    out_y = pltpu.make_async_copy(y1, y_out.at[0], out_sem.at[0])
    out_dh = pltpu.make_async_copy(dh1, dh_out.at[0], out_sem.at[1])
    out_y.start()
    out_dh.start()

    own_hg.wait()
    for copy in xhg + xdu0 + xdu1:
        copy.wait_recv()
    keep_down = pl.ds(pl.multiple_of(k * 32, 32), width // n_dp)
    for s in (2, 3, 0, 1):
        factors = jnp.concatenate([hgr[q, s] for q in range(n_dp)], axis=0)
        gd[s] = tn(factors, all_rows(dur, s))
        if s >= 2:
            msd[s - 2] = gd[s, keep_down, :].astype(BF16)
        if s == 3:
            md = send(msd, mrd, MIRROR + 1, pipe=mirror)
    mu.wait_recv()
    for j in range(2):
        gou[j] = gu[j, keep_up, :] + mru[j].astype(F32)
    out_gu = pltpu.make_async_copy(gou, gu_out.at[0], out_sem.at[2])
    out_gu.start()
    md.wait_recv()
    for j in range(2):
        god[j] = gd[j, keep_down, :] + mrd[j].astype(F32)
    out_gd = pltpu.make_async_copy(god, gd_out.at[0], out_sem.at[3])
    out_gd.start()

    for copy in pending + [mu, md]:
        copy.wait_send()
    for s in range(slots):
        drain("y", s)
        drain("d", s)
    for copy in (out_y, out_dh, out_gu, out_gd):
        copy.wait()


def solution(mesh):
    n_pipe, n_tensor, n_dp = (mesh.shape[a] for a in ("pipe", "tensor", "dp"))

    def per_device(wd, wu, g, x, h, dy, fresh, latest):
        _, slots, width, rank = wd.shape
        rows = x.shape[2]
        half = rows // 2
        chunks = n_tensor
        any_spec = pl.BlockSpec(memory_space=pl.ANY)
        v = pltpu.VMEM
        return pl.pallas_call(
            functools.partial(kernel, n_pipe, n_tensor, n_dp, width * n_tensor),
            out_shape=(
                jax.ShapeDtypeStruct((1, slots, rows, width), BF16),
                jax.ShapeDtypeStruct((1, slots, rows, width), BF16),
                jax.ShapeDtypeStruct((1, 2, width // n_dp, rank), F32),
                jax.ShapeDtypeStruct((1, 2, rank // n_dp, width), F32),
            ),
            in_specs=[any_spec] * 8,
            out_specs=(any_spec,) * 4,
            scratch_shapes=[
                v((slots, width, rank), BF16), v((slots, rank, width), BF16), v((slots, width), F32),
                v((slots, rows, width), BF16), v((2, slots, rows, width), BF16), v((slots, rows, width), BF16),
                v((2, rows, width), BF16), v((2, rows, width), BF16),
                v((slots, 2 * rows, width), BF16),
                v((chunks, half, 3 * rank + 128), BF16), v((chunks, half, 3 * rank + 128), BF16),
                v((chunks, half, rank), BF16), v((chunks, half, rank), BF16),
                v((chunks, half, 2 * rank + 128), BF16), v((chunks, half, 2 * rank), BF16),
                v((chunks, half, 2 * rank + 128), BF16), v((chunks, half, 2 * rank + 128), BF16),
                v((chunks, half, 2 * rank + 128), BF16),
                v((slots, rows, width), BF16), v((slots, rows, width), BF16),
                v((slots, rows, width), BF16), v((slots, rows, width), BF16),
                v((n_dp, slots, 2 * rows, 256), BF16),
                v((n_dp, 2, slots, rows, width), BF16),
                v((n_dp, 2, chunks, half, 128), BF16),
                v((n_dp, 2, chunks, half, rank), BF16),
                v((slots, 256, rank), F32), v((slots, 128, width), F32),
                v((2, width // n_dp, rank), BF16), v((2, rank // n_dp, width), BF16),
                v((2, width // n_dp, rank), BF16), v((2, rank // n_dp, width), BF16),
                v((slots, rows, width), BF16), v((slots, rows, width), BF16),
                v((2, width // n_dp, rank), F32), v((2, rank // n_dp, width), F32),
                pltpu.SemaphoreType.DMA((9,)), pltpu.SemaphoreType.DMA((3,)), pltpu.SemaphoreType.DMA((4,)),
                pltpu.SemaphoreType.DMA((N_SEMS,)), pltpu.SemaphoreType.DMA((N_SEMS,)),
            ],
            compiler_params=pltpu.CompilerParams(
                collective_id=0, has_side_effects=True, vmem_limit_bytes=60 * 2**20
            ),
            name="relay_window",
        )(wd, wu, g, x, h, dy, fresh, latest)

    return jax.shard_map(
        per_device,
        mesh=mesh,
        in_specs=(
            P("pipe", None, "tensor", None),
            P("pipe", None, None, "tensor"),
            P("pipe", None, "tensor"),
            P("pipe", None, "dp", "tensor"),
            P(None, "pipe", None, "dp", "tensor"),
            P("pipe", None, "dp", "tensor"),
            P(None, None, "dp", "tensor"),
            P(None, None, "dp", "tensor"),
        ),
        out_specs=(
            P("pipe", None, "dp", "tensor"),
            P("pipe", None, "dp", "tensor"),
            P("pipe", None, ("tensor", "dp"), None),
            P("pipe", None, "dp", "tensor"),
        ),
        check_vma=False,
    )
```

time: 506 us -> 123 us (0.24)
  the two profiles are of different devices: /device:TPU:88 before, /device:TPU:128 now
where the time goes in v1:
time: 123 us
  Pallas kernels  116 us (94%)
  local copies, waits for them, and re-layouts  5.68 us (5%)
    pallas_call x1, Pallas kernels, per_device(): pl.pallas_call(functools.partial(kernel, n_pipe, n_tensor, n_dp, width *...  116 us
    unnamed x6, local copies, waits for them, and re-layouts  5.68 us

profile of v1, /device:TPU:128, one launch (start us, length us, event | category | flops | bytes accessed | tf_op | source)
XLA Modules:
  0.0 122.6 jit_solution(1787951472637909688)
XLA Ops:
  0.6 116.3 %relay_window.1 = (bf16[1,4,32,640]{3,2,1,0:T(8,128)(2,1)}, bf16[1,4,32,640]{3,2,1,0:T(8,128)(2,1)}, f32[1,2,160,256]{3,2,1,0:T(8,128)}, f32[1,2,64,640]{3,2,1,0:T(8,128)}) custom-call(bf16[1,4,640,256]{3,2,1,0:T(8,128)(2,1)} %wd_hbm.1, bf16[1,4,256,640]{3,2,1,0:T(8,128)(2,1)} %wu_hbm.1, f32[1,4,640]{2,1,0:T(4,128)} %g_hbm.1, bf16[1,4,32,640]{3,2,1,0:T(8,128)(2,1)} %x_hbm.1, ...), custom_call_target="tpu_custom_call" | custom-call | tf_op jit(solution)/shard_map/relay_window/pallas_call | solution.py:395
  116.9 0.0 copy-start
  117.0 1.6 %copy.16 = bf16[1,4,32,640]{3,2,1,0:T(8,128)(2,1)} copy(bf16[1,4,32,640]{3,2,1,0:T(8,128)(2,1)} %get-tuple-element.8) | data formatting | bytes 327680
  118.6 1.6 %copy.17 = bf16[1,4,32,640]{3,2,1,0:T(8,128)(2,1)} copy(bf16[1,4,32,640]{3,2,1,0:T(8,128)(2,1)} %get-tuple-element.9) | data formatting | bytes 327680
  120.2 1.7 %copy.18 = f32[1,2,160,256]{3,2,1,0:T(8,128)} copy(f32[1,2,160,256]{3,2,1,0:T(8,128)} %get-tuple-element.10) | data formatting | bytes 655360
  121.9 0.0 copy-done
  121.9 0.7 copy.19
Async XLA Ops:
  116.9 5.0 %copy-start = (f32[1,2,64,640]{3,2,1,0:T(8,128)S(1)}, f32[1,2,64,640]{3,2,1,0:T(8,128)}, u32[]{:S(2)}) copy-start(f32[1,2,64,640]{3,2,1,0:T(8,128)} %get-tuple-element.11) | copy-start | bytes 983044

commit v2 on v1

v2 whole, which is shorter than its diff:
```python
import functools

import jax
import jax.numpy as jnp
from jax import lax
from jax.experimental import pallas as pl
from jax.experimental.pallas import tpu as pltpu
from jax.sharding import PartitionSpec as P

MESH = pl.DeviceIdType.MESH
EPS = 1e-06
F32 = jnp.float32
BF16 = jnp.bfloat16

FAMILIES = {
    "rs1b": 8, "rs1f": 8, "rs1h": 8, "sq1": 8, "ag1b": 8, "ds1": 8, "ag1f": 8, "ag1a": 8,
    "rs2b": 8, "rs2f": 8, "sq2": 8, "ag2b": 8, "ds2": 8, "ag2f": 8, "up": 4, "down": 4,
    "hg": 4, "dy0": 4, "dy1": 16, "a": 8, "du0": 4, "du1": 4, "mirror": 3,
}
INDEX = {}
N_SEMS = 0
for _name, _count in FAMILIES.items():
    INDEX[_name] = N_SEMS
    N_SEMS += _count


def nt(a, b):
    return lax.dot_general(a, b, (((1,), (1,)), ((), ())), preferred_element_type=F32)


def tn(a, b):
    return lax.dot_general(a, b, (((0,), (0,)), ((), ())), preferred_element_type=F32)


def nn(a, b):
    return jnp.dot(a, b, preferred_element_type=F32)


def packed(*columns):
    rows = columns[0].shape[0]
    lane = lax.broadcasted_iota(jnp.int32, (rows, 128), 1)
    row = lax.broadcasted_iota(jnp.int32, (rows, 128), 0)
    out = jnp.zeros((rows, 128), F32)
    for i, column in enumerate(columns):
        out = jnp.where(lane == row + i * rows, column, out)
    return jnp.sum(out, axis=0, keepdims=True)


def unpacked(line, rows, i):
    lane = lax.broadcasted_iota(jnp.int32, (rows, 128), 1)
    row = lax.broadcasted_iota(jnp.int32, (rows, 128), 0)
    return jnp.sum(jnp.where(lane == row + i * rows, line, 0.0), axis=1, keepdims=True)


def kernel(
    n_pipe, n_tensor, n_dp, d_model,
    wd_hbm, wu_hbm, g_hbm, x_hbm, h_hbm, dy_hbm, fresh_hbm, latest_hbm,
    y_out, dh_out, gd_out, gu_out,
    wd, wu, g, x0, h, dy0, fresh, latest, hg,
    s1b, r1b, s1f, r1f, s1h, r1h, sq1, rq1, a1b, d1, a1f, a1a,
    s2b, r2b, s2f, r2f, sq2, rq2, a2b, d2, a2f,
    ys, ds, x1, dy1, hgr, dyr, ar, dur, gd, gu, msd, msu, mrd, mru,
    in_sem, own_sem, send_sem, recv_sem, ready,
):
    p = lax.axis_index("pipe")
    t = lax.axis_index("tensor")
    k = lax.axis_index("dp")
    last = n_pipe - 1
    middle = n_pipe // 2
    slots, rows, width = x0.shape
    rank = wd.shape[2]
    half = rows // 2
    not_first, not_last = p > 0, p < last
    upper = p >= middle
    lower = p < middle
    mirror = last - p

    barrier = pltpu.get_barrier_semaphore()

    def greet(**where):
        pl.semaphore_signal(barrier, inc=1, device_id=where, device_id_type=MESH)

    @pl.when(lower)
    def _():
        greet(pipe=mirror)

    for j in range(1, n_tensor):
        greet(tensor=lax.rem(t + j, n_tensor))

    @pl.when(jnp.logical_and(not_first, p != middle))
    def _():
        greet(pipe=p - 1)

    @pl.when(not_last)
    def _():
        greet(pipe=p + 1)

    for j in range(1, n_dp):
        greet(dp=lax.rem(k + j, n_dp))

    def load(i, src, dst):
        copy = pltpu.make_async_copy(src, dst, in_sem.at[i])
        copy.start()
        return copy

    order = [lax.rem(t // 2 + i, slots) for i in (2, 1, 3, 0)]
    first = [load(0, x_hbm.at[0], x0), load(1, h_hbm.at[0, 0], h.at[0]), load(2, h_hbm.at[1, 0], h.at[1]),
             load(3, g_hbm.at[0], g)]
    by_slot = []
    for i, s in enumerate(order):
        pair = [load(4 + 2 * i, wd_hbm.at[0, s], wd.at[s]), load(5 + 2 * i, wu_hbm.at[0, s], wu.at[s])]
        if i == 0:
            pair.append(load(12, dy_hbm.at[0], dy0))
        by_slot.append(pair)
    entering = [load(13, fresh_hbm.at[0], fresh), load(14, latest_hbm.at[0], latest)]

    pending = []

    def remote(src, dst, index, **where):
        return pltpu.make_async_remote_copy(
            src_ref=src, dst_ref=dst, send_sem=send_sem.at[index], recv_sem=recv_sem.at[index],
            device_id=where, device_id_type=MESH,
        )

    ring = [4, 3, 5, 2, 6, 1, 7] if n_tensor == 8 else list(range(1, n_tensor))
    near = list(range(1, n_dp))

    class Exchange:
        def __init__(self, family, axis, src_of, dst, offset=0):
            me, count, self.steps = (t, n_tensor, ring) if axis == "tensor" else (k, n_dp, near)
            self.base, self.axis, self.src_of, self.dst = INDEX[family] + offset, axis, src_of, dst
            self.me, self.count = me, count
            pending.append(self)

        def copy(self, peer, j):
            return remote(self.src_of(peer), self.dst, self.base + j, **{self.axis: peer})

        def start_to(self, peer):
            self.copy(peer, lax.rem(peer - self.me + self.count, self.count)).start()

        def start(self):
            for j in self.steps:
                self.copy(lax.rem(self.me + j, self.count), j).start()
            return self

        def received(self):
            for j in self.steps:
                self.copy(lax.rem(self.me + j, self.count), j).wait_recv()
                yield lax.rem(self.me + self.count - j, self.count)

        def receive(self):
            for _ in self.received():
                pass

        def drain(self):
            for j in self.steps:
                self.copy(lax.rem(self.me + j, self.count), j).wait_send()

    def scatter(family, src, dst):
        return Exchange(family, "tensor", lambda peer: src.at[peer], dst.at[t])

    def gather(family, ref):
        return Exchange(family, "tensor", lambda peer: ref.at[t], ref.at[t])

    def summed(exchange, src, dst):
        total = src[t].astype(F32)
        for q in exchange.received():
            total = total + dst[q].astype(F32)
        return total

    rs1b, rs1f, rs1h = scatter("rs1b", s1b, r1b), scatter("rs1f", s1f, r1f), scatter("rs1h", s1h, r1h)
    xsq1 = scatter("sq1", sq1, rq1)
    for copy in first:
        copy.wait()
    for n, s in enumerate(order):
        gain = g[pl.ds(s, 1), :]
        xf, h0f, h1f = x0[s].astype(F32), h[0, s].astype(F32), h[1, s].astype(F32)
        h0s, h1s = (h0f * gain).astype(BF16), (h1f * gain).astype(BF16)
        hg[s, 0:rows] = h0s
        hg[s, rows : 2 * rows] = h1s
        stacked = jnp.concatenate([h0s, (xf * gain).astype(BF16), h1s], axis=0)
        for copy in by_slot[n]:
            copy.wait()
        part = nn(stacked, wd[s]).astype(BF16)
        grad = nt(dy0[s], wu[s]).astype(BF16)
        sums = [jnp.sum(v * v, axis=1, keepdims=True) for v in (xf, h0f, h1f)]
        for i in range(2):
            lo, hi = i * half, (i + 1) * half
            r = 2 * s + i
            s1b[r, :, 0:rank] = part[lo:hi]
            s1b[r, :, rank : 2 * rank] = grad[lo:hi]
            s1f[r] = part[rows + lo : rows + hi]
            s1h[r] = part[2 * rows + lo : 2 * rows + hi]
            sq1[r] = packed(*[v[lo:hi] for v in sums])
        if n == 0:
            count = n_tensor - 1 + n_dp - 1 + not_first.astype(jnp.int32) + not_last.astype(jnp.int32)
            count = count + upper.astype(jnp.int32) - (p == middle - 1).astype(jnp.int32)
            pl.semaphore_wait(barrier, count)
        for peer in ([2 * s, 2 * s + 1] if n < slots - 1 else [t + 1 - 2 * lax.rem(t, 2)]):
            xsq1.start_to(peer)
            rs1b.start_to(peer)
    rs1f.start()
    rs1h.start()

    @pl.when(upper)
    def _():
        pl.semaphore_signal(ready.at[0], inc=1, device_id={"pipe": mirror}, device_id_type=MESH)

    @pl.when(p == middle)
    def _():
        pl.semaphore_signal(ready.at[1], inc=1, device_id={"pipe": p - 1}, device_id_type=MESH)

    def window(peer):
        return hg.at[:, :, pl.ds(pl.multiple_of(peer * 128, 128), 256)]

    xhg = Exchange("hg", "dp", window, hgr.at[k]).start()
    xdy0 = Exchange("dy0", "dp", lambda peer: dy0, dyr.at[k, 0]).start()
    own_hg = pltpu.make_async_copy(window(k), hgr.at[k], own_sem.at[0])
    own_hg.start()
    dyr[k, 0] = dy0[...]

    @pl.when(jnp.logical_not(not_first))
    def _():
        entering[0].wait()
        entering[1].wait()
        x1[0] = fresh[0]
        dy1[1] = latest[0]

    @pl.when(jnp.logical_not(not_last))
    def _():
        entering[0].wait()
        entering[1].wait()
        x1[2] = fresh[1]
        dy1[3] = latest[1]

    @pl.when(jnp.logical_and(not_first, not_last))
    def _():
        entering[0].wait()
        entering[1].wait()

    def factor_of(column):
        return 1.0 / jnp.sqrt(column / d_model + EPS)

    def back(latent, factor, da):
        z = latent * factor
        sig = jax.nn.sigmoid(z)
        dz = da * sig * (1.0 + z * (1.0 - sig))
        dss = -0.5 * factor * factor * factor / d_model * jnp.sum(dz * latent, axis=1, keepdims=True)
        return (z * sig).astype(BF16), (dz * factor).astype(BF16), packed(dss)

    def swish(z):
        return (z * jax.nn.sigmoid(z)).astype(BF16)

    squares = summed(xsq1, sq1, rq1)
    fx, f0, f1 = (factor_of(unpacked(squares, half, i)) for i in range(3))
    total = summed(rs1b, s1b, r1b)
    ah0, du0, dss0 = back(total[:, 0:rank], f0, total[:, rank : 2 * rank])
    a1b[t] = du0
    d1[t] = dss0
    ag1b = gather("ag1b", a1b).start()
    xds1 = gather("ds1", d1).start()
    a1f[t] = swish(summed(rs1f, s1f, r1f) * fx)
    ag1f = gather("ag1f", a1f).start()
    u1 = summed(rs1h, s1h, r1h)
    a1a[t, :, 0:rank] = ah0
    a1a[t, :, rank : 2 * rank] = swish(u1 * f1)
    ag1a = gather("ag1a", a1a).start()

    def both(ref, s):
        return jnp.concatenate([ref[2 * s], ref[2 * s + 1]], axis=0)

    def dh_of(a_ref, d_ref, s, kept, cot):
        dss = jnp.concatenate([unpacked(d_ref[2 * s + i], half, 0) for i in range(2)], axis=0)
        feature = nt(both(a_ref, s), wd[s]) * g[s : s + 1, :]
        return (feature + 2.0 * kept.astype(F32) * dss + cot.astype(F32)).astype(BF16)

    def y_of(a_ref, s, rows_in):
        return (rows_in.astype(F32) + nn(both(a_ref, s), wu[s])).astype(BF16)

    up_index = {("y", 0): 0, ("y", 3): 1, ("d", 1): 2, ("d", 2): 3}
    down_index = {("y", 1): 0, ("y", 2): 1, ("d", 0): 2, ("d", 3): 3}

    def shift(kind, s):
        src, dst = (ys.at[s], x1.at[s]) if kind == "y" else (ds.at[s], dy1.at[s])
        if (kind, s) in up_index:
            copy = remote(src, dst, INDEX["up"] + up_index[kind, s], pipe=p + 1)
            return not_last, not_first, copy
        copy = remote(src, dst, INDEX["down"] + down_index[kind, s], pipe=p - 1)
        return not_first, not_last, copy

    def start_shift(kind, s):
        can_send, _, copy = shift(kind, s)
        pl.when(can_send)(copy.start)

    def land(kind, s):
        _, can_receive, copy = shift(kind, s)
        pl.when(can_receive)(copy.wait_recv)

    def drain(kind, s):
        can_send, _, copy = shift(kind, s)
        pl.when(can_send)(copy.wait_send)

    ag1b.receive()
    xds1.receive()

    @pl.when(p == middle - 1)
    def _():
        pl.semaphore_wait(ready.at[1], 1)

    for s in (2, 3, 0, 1):
        ds[s] = dh_of(a1b, d1, s, h[0, s], dy0[s])
        start_shift("d", s)
    xdu0 = Exchange("du0", "dp", lambda peer: a1b, dur.at[k, 0]).start()
    dur[k, 0] = a1b[...]

    @pl.when(jnp.logical_not(not_first))
    def _():
        dy1[2] = ds[3]

    @pl.when(jnp.logical_not(not_last))
    def _():
        dy1[0] = ds[1]

    ag1f.receive()
    for s in range(slots):
        ys[s] = y_of(a1f, s, x0[s])
        start_shift("y", s)

    @pl.when(jnp.logical_not(not_first))
    def _():
        x1[3] = ys[2]

    @pl.when(jnp.logical_not(not_last))
    def _():
        x1[1] = ys[0]

    rs2b, rs2f = scatter("rs2b", s2b, r2b), scatter("rs2f", s2f, r2f)
    xsq2 = scatter("sq2", sq2, rq2)
    xdy1 = []
    for s in (2, 3, 0, 1):
        land("d", s)
        grad = nt(dy1[s], wu[s]).astype(BF16)
        for i in range(2):
            r = 2 * s + i
            s2b[r] = grad[i * half : (i + 1) * half]

            @pl.when(t != r)
            def _():
                rs2b.start_to(r)

        xdy1.append(Exchange("dy1", "dp", lambda peer, s=s: dy1.at[s], dyr.at[k, 1, s], 4 * s).start())
    dyr[k, 1] = dy1[...]
    for s in range(slots):
        land("y", s)
        xf = x1[s].astype(F32)
        part = nn((xf * g[s : s + 1, :]).astype(BF16), wd[s]).astype(BF16)
        squares = jnp.sum(xf * xf, axis=1, keepdims=True)
        for i in range(2):
            lo, hi = i * half, (i + 1) * half
            s2f[2 * s + i] = part[lo:hi]
            sq2[2 * s + i] = packed(squares[lo:hi])
    xsq2.start()
    rs2f.start()

    ag1a.receive()

    def latents(peer, tick):
        return a1a.at[:, :, pl.ds(pl.multiple_of(tick * rank + peer // 2 * 128, 128), 128)]

    xa = [
        Exchange("a", "dp", functools.partial(latents, tick=tick), ar.at[k, tick], 4 * tick).start()
        for tick in range(2)
    ]
    own_a = [pltpu.make_async_copy(latents(k, tick), ar.at[k, tick], own_sem.at[1 + tick]) for tick in range(2)]
    for copy in own_a:
        copy.start()

    _, du1, dss1 = back(u1, f1, summed(rs2b, s2b, r2b))
    a2b[t] = du1
    d2[t] = dss1
    ag2b = gather("ag2b", a2b).start()
    xds2 = gather("ds2", d2).start()

    for copy in own_a:
        copy.wait()
    for exchange in [xdy0] + xdy1 + xa:
        exchange.receive()

    @pl.when(lower)
    def _():
        pl.semaphore_wait(ready.at[0], 1)

    def all_rows(ref, s):
        return jnp.concatenate(
            [ref[q, tick, 2 * s + i] for q in range(n_dp) for tick in range(2) for i in range(2)], axis=0
        )

    def up_gradient(s):
        cot = jnp.concatenate([dyr[q, tick, s] for q in range(n_dp) for tick in range(2)], axis=0)
        return tn(all_rows(ar, s), cot)

    keep_up = pl.ds(pl.multiple_of(lax.rem(k, 2) * 64, 64), 64)
    for s in (2, 3):
        gu[s] = up_gradient(s)
        msu[s - 2] = gu[s, keep_up, :].astype(BF16)
    mu = remote(msu, mru, INDEX["mirror"], pipe=mirror)
    mu.start()

    ag2b.receive()
    xds2.receive()
    xdu1 = Exchange("du1", "dp", lambda peer: a2b, dur.at[k, 1]).start()
    dur[k, 1] = a2b[...]
    squares = summed(xsq2, sq2, rq2)
    a2f[t] = swish(summed(rs2f, s2f, r2f) * factor_of(unpacked(squares, half, 0)))
    ag2f = gather("ag2f", a2f).start()

    own_hg.wait()
    for exchange in (xhg, xdu0, xdu1):
        exchange.receive()
    keep_down = pl.ds(pl.multiple_of(k * 32, 32), width // n_dp)

    def down_gradient(s):
        factors = jnp.concatenate([hgr[q, s] for q in range(n_dp)], axis=0)
        return tn(factors, all_rows(dur, s))

    md = []
    for s in (2, 3):
        gd[s] = down_gradient(s)
        msd[s - 2] = gd[s, keep_down, :].astype(BF16)
        md.append(remote(msd.at[s - 2], mrd.at[s - 2], INDEX["mirror"] + s - 1, pipe=mirror))
        md[-1].start()
    for s in (0, 1):
        gu[s] = up_gradient(s)
        gd[s] = down_gradient(s)
    for s in range(slots):
        dh_out[0, s] = dh_of(a2b, d2, s, h[1, s], dy1[s])
    ag2f.receive()
    for s in range(slots):
        y_out[0, s] = y_of(a2f, s, x1[s])
    mu.wait_recv()
    for j in range(2):
        gu_out[0, j] = gu[j, keep_up, :] + mru[j].astype(F32)
    for j in range(2):
        md[j].wait_recv()
        gd_out[0, j] = gd[j, keep_down, :] + mrd[j].astype(F32)

    for exchange in pending:
        exchange.drain()
    for copy in [mu] + md:
        copy.wait_send()
    for s in range(slots):
        drain("y", s)
        drain("d", s)


def solution(mesh):
    n_pipe, n_tensor, n_dp = (mesh.shape[a] for a in ("pipe", "tensor", "dp"))

    def per_device(wd, wu, g, x, h, dy, fresh, latest):
        _, slots, width, rank = wd.shape
        rows = x.shape[2]
        half = rows // 2
        chunks = n_tensor
        any_spec = pl.BlockSpec(memory_space=pl.ANY)
        vmem_spec = pl.BlockSpec(memory_space=pltpu.VMEM)
        v = pltpu.VMEM
        shapes = [
            ((1, slots, rows, width), BF16), ((1, slots, rows, width), BF16),
            ((1, 2, width // n_dp, rank), F32), ((1, 2, rank // n_dp, width), F32),
        ]

        def chunk(columns):
            return v((chunks, half, columns), BF16)

        line = v((chunks, 1, 128), F32)
        act = v((slots, rows, width), BF16)
        results = pl.pallas_call(
            functools.partial(kernel, n_pipe, n_tensor, n_dp, width * n_tensor),
            out_shape=tuple(v(*shape) for shape in shapes),
            in_specs=[any_spec] * 8,
            out_specs=(vmem_spec,) * 4,
            scratch_shapes=[
                v((slots, width, rank), BF16), v((slots, rank, width), BF16), v((slots, width), F32),
                act, v((2, slots, rows, width), BF16), act,
                v((2, rows, width), BF16), v((2, rows, width), BF16),
                v((slots, 2 * rows, width), BF16),
                chunk(2 * rank), chunk(2 * rank), chunk(rank), chunk(rank), chunk(rank), chunk(rank),
                line, line, chunk(rank), line, chunk(rank), chunk(2 * rank),
                chunk(rank), chunk(rank), chunk(rank), chunk(rank), line, line, chunk(rank), line, chunk(rank),
                act, act, act, act,
                v((n_dp, slots, 2 * rows, 256), BF16),
                v((n_dp, 2, slots, rows, width), BF16),
                v((n_dp, 2, chunks, half, 128), BF16),
                v((n_dp, 2, chunks, half, rank), BF16),
                v((slots, 256, rank), F32), v((slots, 128, width), F32),
                v((2, width // n_dp, rank), BF16), v((2, rank // n_dp, width), BF16),
                v((2, width // n_dp, rank), BF16), v((2, rank // n_dp, width), BF16),
                pltpu.SemaphoreType.DMA((15,)), pltpu.SemaphoreType.DMA((3,)),
                pltpu.SemaphoreType.DMA((N_SEMS,)), pltpu.SemaphoreType.DMA((N_SEMS,)),
                pltpu.SemaphoreType.REGULAR((2,)),
            ],
            compiler_params=pltpu.CompilerParams(
                collective_id=0, has_side_effects=True, vmem_limit_bytes=60 * 2**20
            ),
            name="relay_window",
        )(wd, wu, g, x, h, dy, fresh, latest)
        return results

    return jax.shard_map(
        per_device,
        mesh=mesh,
        in_specs=(
            P("pipe", None, "tensor", None),
            P("pipe", None, None, "tensor"),
            P("pipe", None, "tensor"),
            P("pipe", None, "dp", "tensor"),
            P(None, "pipe", None, "dp", "tensor"),
            P("pipe", None, "dp", "tensor"),
            P(None, None, "dp", "tensor"),
            P(None, None, "dp", "tensor"),
        ),
        out_specs=(
            P("pipe", None, "dp", "tensor"),
            P("pipe", None, "dp", "tensor"),
            P("pipe", None, ("tensor", "dp"), None),
            P("pipe", None, "dp", "tensor"),
        ),
        check_vma=False,
    )
```

time: 123 us -> 112 us (0.911)
  the two profiles are of different devices: /device:TPU:128 before, /device:TPU:81 now
where the time goes in v2:
time: 112 us
  Pallas kernels  109 us (97%)
  local copies, waits for them, and re-layouts  2.78 us (2%)
    pallas_call x1, Pallas kernels, per_device(): pl.pallas_call(functools.partial(kernel, n_pipe, n_tensor, n_dp, width *...  109 us
    unnamed x4, local copies, waits for them, and re-layouts  2.78 us

profile of v2, /device:TPU:81, one launch (start us, length us, event | category | flops | bytes accessed | tf_op | source)
XLA Modules:
  0.0 112.3 jit_solution(16563870393217441868)
XLA Ops:
  0.6 108.9 %relay_window.1 = (bf16[1,4,32,640]{3,2,1,0:T(8,128)(2,1)S(1)}, bf16[1,4,32,640]{3,2,1,0:T(8,128)(2,1)S(1)}, f32[1,2,160,256]{3,2,1,0:T(8,128)S(1)}, f32[1,2,64,640]{3,2,1,0:T(8,128)S(1)}) custom-call(bf16[1,4,640,256]{3,2,1,0:T(8,128)(2,1)} %wd_hbm.1, bf16[1,4,256,640]{3,2,1,0:T(8,128)(2,1)} %wu_hbm.1, f32[1,4,640]{2,1,0:T(4,128)} %g_hbm.1, ...), custom_call_target="tpu_custom_call" | custom-call | tf_op jit(solution)/shard_map/relay_window/pallas_call | solution.py:477
  109.5 0.7 copy.16
  110.2 0.7 copy.17
  110.9 0.7 copy.18
  111.6 0.7 copy.19

commit v3 on v2

--- a/solution.py
+++ b/solution.py
@@ -199,8 +199,6 @@
         for peer in ([2 * s, 2 * s + 1] if n < slots - 1 else [t + 1 - 2 * lax.rem(t, 2)]):
             xsq1.start_to(peer)
             rs1b.start_to(peer)
-    rs1f.start()
-    rs1h.start()
 
     @pl.when(upper)
     def _():
@@ -259,12 +257,8 @@
     d1[t] = dss0
     ag1b = gather("ag1b", a1b).start()
     xds1 = gather("ds1", d1).start()
-    a1f[t] = swish(summed(rs1f, s1f, r1f) * fx)
-    ag1f = gather("ag1f", a1f).start()
-    u1 = summed(rs1h, s1h, r1h)
-    a1a[t, :, 0:rank] = ah0
-    a1a[t, :, rank : 2 * rank] = swish(u1 * f1)
-    ag1a = gather("ag1a", a1a).start()
+    rs1f.start()
+    rs1h.start()
 
     def both(ref, s):
         return jnp.concatenate([ref[2 * s], ref[2 * s + 1]], axis=0)
@@ -321,18 +315,12 @@
     def _():
         dy1[0] = ds[1]
 
-    ag1f.receive()
-    for s in range(slots):
-        ys[s] = y_of(a1f, s, x0[s])
-        start_shift("y", s)
-
-    @pl.when(jnp.logical_not(not_first))
-    def _():
-        x1[3] = ys[2]
-
-    @pl.when(jnp.logical_not(not_last))
-    def _():
-        x1[1] = ys[0]
+    a1f[t] = swish(summed(rs1f, s1f, r1f) * fx)
+    ag1f = gather("ag1f", a1f).start()
+    u1 = summed(rs1h, s1h, r1h)
+    a1a[t, :, 0:rank] = ah0
+    a1a[t, :, rank : 2 * rank] = swish(u1 * f1)
+    ag1a = gather("ag1a", a1a).start()
 
     rs2b, rs2f = scatter("rs2b", s2b, r2b), scatter("rs2f", s2f, r2f)
     xsq2 = scatter("sq2", sq2, rq2)
@@ -350,6 +338,63 @@
 
         xdy1.append(Exchange("dy1", "dp", lambda peer, s=s: dy1.at[s], dyr.at[k, 1, s], 4 * s).start())
     dyr[k, 1] = dy1[...]
+    ag1f.receive()
+    for s in range(slots):
+        ys[s] = y_of(a1f, s, x0[s])
+        start_shift("y", s)
+
+    @pl.when(jnp.logical_not(not_first))
+    def _():
+        x1[3] = ys[2]
+
+    @pl.when(jnp.logical_not(not_last))
+    def _():
+        x1[1] = ys[0]
+
+    ag1a.receive()
+
+    def latents(peer, tick):
+        return a1a.at[:, :, pl.ds(pl.multiple_of(tick * rank + peer // 2 * 128, 128), 128)]
+
+    xa = [
+        Exchange("a", "dp", functools.partial(latents, tick=tick), ar.at[k, tick], 4 * tick).start()
+        for tick in range(2)
+    ]
+    own_a = [pltpu.make_async_copy(latents(k, tick), ar.at[k, tick], own_sem.at[1 + tick]) for tick in range(2)]
+    for copy in own_a:
+        copy.start()
+
+    _, du1, dss1 = back(u1, f1, summed(rs2b, s2b, r2b))
+    a2b[t] = du1
+    d2[t] = dss1
+    ag2b = gather("ag2b", a2b).start()
+    xds2 = gather("ds2", d2).start()
+
+    for copy in own_a:
+        copy.wait()
+    for exchange in [xdy0] + xdy1 + xa:
+        exchange.receive()
+
+    @pl.when(lower)
+    def _():
+        pl.semaphore_wait(ready.at[0], 1)
+
+    def all_rows(ref, s):
+        return jnp.concatenate(
+            [ref[q, tick, 2 * s + i] for q in range(n_dp) for tick in range(2) for i in range(2)], axis=0
+        )
+
+    def up_gradient(s):
+        cot = jnp.concatenate([dyr[q, tick, s] for q in range(n_dp) for tick in range(2)], axis=0)
+        return tn(all_rows(ar, s), cot)
+
+    keep_up = pl.ds(pl.multiple_of(lax.rem(k, 2) * 64, 64), 64)
+    for s in (2, 3):
+        gu[s] = up_gradient(s)
+        msu[s - 2] = gu[s, keep_up, :].astype(BF16)
+    mu = remote(msu, mru, INDEX["mirror"], pipe=mirror)
+    mu.start()
+
     for s in range(slots):
         land("y", s)
         xf = x1[s].astype(F32)
@@ -362,58 +407,10 @@
     xsq2.start()
     rs2f.start()
 
-    ag1a.receive()
-
-    def latents(peer, tick):
-        return a1a.at[:, :, pl.ds(pl.multiple_of(tick * rank + peer // 2 * 128, 128), 128)]
-
-    xa = [
-        Exchange("a", "dp", functools.partial(latents, tick=tick), ar.at[k, tick], 4 * tick).start()
-        for tick in range(2)
-    ]
-    own_a = [pltpu.make_async_copy(latents(k, tick), ar.at[k, tick], own_sem.at[1 + tick]) for tick in range(2)]
-    for copy in own_a:
-        copy.start()
-
-    _, du1, dss1 = back(u1, f1, summed(rs2b, s2b, r2b))
-    a2b[t] = du1
-    d2[t] = dss1
-    ag2b = gather("ag2b", a2b).start()
-    xds2 = gather("ds2", d2).start()
-
-    for copy in own_a:
-        copy.wait()
-    for exchange in [xdy0] + xdy1 + xa:
-        exchange.receive()
-
-    @pl.when(lower)
-    def _():
-        pl.semaphore_wait(ready.at[0], 1)
-
-    def all_rows(ref, s):
-        return jnp.concatenate(
-            [ref[q, tick, 2 * s + i] for q in range(n_dp) for tick in range(2) for i in range(2)], axis=0
-        )
-
-    def up_gradient(s):
-        cot = jnp.concatenate([dyr[q, tick, s] for q in range(n_dp) for tick in range(2)], axis=0)
-        return tn(all_rows(ar, s), cot)
-
-    keep_up = pl.ds(pl.multiple_of(lax.rem(k, 2) * 64, 64), 64)
-    for s in (2, 3):
-        gu[s] = up_gradient(s)
-        msu[s - 2] = gu[s, keep_up, :].astype(BF16)
-    mu = remote(msu, mru, INDEX["mirror"], pipe=mirror)
-    mu.start()
-
     ag2b.receive()
     xds2.receive()
     xdu1 = Exchange("du1", "dp", lambda peer: a2b, dur.at[k, 1]).start()
     dur[k, 1] = a2b[...]
-    squares = summed(xsq2, sq2, rq2)
-    a2f[t] = swish(summed(rs2f, s2f, r2f) * factor_of(unpacked(squares, half, 0)))
-    ag2f = gather("ag2f", a2f).start()
-
     own_hg.wait()
     for exchange in (xhg, xdu0, xdu1):
         exchange.receive()
@@ -429,6 +426,9 @@
         msd[s - 2] = gd[s, keep_down, :].astype(BF16)
         md.append(remote(msd.at[s - 2], mrd.at[s - 2], INDEX["mirror"] + s - 1, pipe=mirror))
         md[-1].start()
+    squares = summed(xsq2, sq2, rq2)
+    a2f[t] = swish(summed(rs2f, s2f, r2f) * factor_of(unpacked(squares, half, 0)))
+    ag2f = gather("ag2f", a2f).start()
     for s in (0, 1):
         gu[s] = up_gradient(s)
         gd[s] = down_gradient(s)

time: 112 us -> 105 us (0.938)
  the two profiles are of different devices: /device:TPU:81 before, /device:TPU:73 now
where the time goes in v3:
time: 105 us; the launch traced here: 104 us
  Pallas kernels  101 us (96%)
  local copies, waits for them, and re-layouts  2.78 us (3%)
    pallas_call x1, Pallas kernels, per_device(): pl.pallas_call(functools.partial(kernel, n_pipe, n_tensor, n_dp, width *...  101 us
    unnamed x4, local copies, waits for them, and re-layouts  2.78 us

profile of v3, /device:TPU:73, one launch (start us, length us, event | category | flops | bytes accessed | tf_op | source)
XLA Modules:
  0.0 104.4 jit_solution(9235652678899048200)
XLA Ops:
  0.6 101.0 %relay_window.1 = (bf16[1,4,32,640]{3,2,1,0:T(8,128)(2,1)S(1)}, bf16[1,4,32,640]{3,2,1,0:T(8,128)(2,1)S(1)}, f32[1,2,160,256]{3,2,1,0:T(8,128)S(1)}, f32[1,2,64,640]{3,2,1,0:T(8,128)S(1)}) custom-call(bf16[1,4,640,256]{3,2,1,0:T(8,128)(2,1)} %wd_hbm.1, bf16[1,4,256,640]{3,2,1,0:T(8,128)(2,1)} %wu_hbm.1, f32[1,4,640]{2,1,0:T(4,128)} %g_hbm.1, ...), custom_call_target="tpu_custom_call" | custom-call | tf_op jit(solution)/shard_map/relay_window/pallas_call | solution.py:477
  101.7 0.7 copy.16
  102.3 0.7 copy.17
  103.0 0.7 copy.18
  103.7 0.7 copy.19

commit v4 on v3

--- a/solution.py
+++ b/solution.py
@@ -451,6 +451,15 @@
     for s in range(slots):
         drain("y", s)
         drain("d", s)
+
+
+def write_kernel(*refs):
+    count = len(refs) // 2
+    copies = [pltpu.make_async_copy(refs[i], refs[count + i], refs[-1].at[i]) for i in range(count)]
+    for copy in copies:
+        copy.start()
+    for copy in copies:
+        copy.wait()
 
 
 def solution(mesh):
@@ -504,7 +513,14 @@
             ),
             name="relay_window",
         )(wd, wu, g, x, h, dy, fresh, latest)
-        return results
+        return pl.pallas_call(
+            write_kernel,
+            out_shape=tuple(jax.ShapeDtypeStruct(*shape) for shape in shapes),
+            in_specs=[vmem_spec] * 4,
+            out_specs=(any_spec,) * 4,
+            scratch_shapes=[pltpu.SemaphoreType.DMA((4,))],
+            name="write_results",
+        )(*[pltpu.with_memory_space_constraint(r, pltpu.VMEM) for r in results])
 
     return jax.shard_map(
         per_device,

time: 105 us -> 103 us (0.981)
  local copies, waits for them, and re-layouts: 2.78 us -> 0 us
    unnamed x4 -> x0, local copies, waits for them, and re-layouts: 2.78 us -> none
where the time goes in v4:
time: 103 us
  Pallas kernels  102 us (99%)
    pallas_call x1, Pallas kernels, per_device(): pl.pallas_call(functools.partial(kernel, n_pipe, n_tensor, n_dp, width *...  101 us

profile of v4, /device:TPU:73, one launch (start us, length us, event | category | flops | bytes accessed | tf_op | source)
XLA Modules:
  0.0 102.6 jit_solution(1601531511899138851)
XLA Ops:
  0.6 101.0 %relay_window.1 = (bf16[1,4,32,640]{3,2,1,0:T(8,128)(2,1)S(1)}, bf16[1,4,32,640]{3,2,1,0:T(8,128)(2,1)S(1)}, f32[1,2,160,256]{3,2,1,0:T(8,128)S(1)}, f32[1,2,64,640]{3,2,1,0:T(8,128)S(1)}) custom-call(bf16[1,4,640,256]{3,2,1,0:T(8,128)(2,1)} %wd_hbm.1, bf16[1,4,256,640]{3,2,1,0:T(8,128)(2,1)} %wu_hbm.1, f32[1,4,640]{2,1,0:T(4,128)} %g_hbm.1, ...), custom_call_target="tpu_custom_call" | custom-call | tf_op jit(solution)/shard_map/relay_window/pallas_call | solution.py:486
  101.7 1.0 write_results.1

commit v5 on v4

--- a/solution.py
+++ b/solution.py
@@ -15,7 +15,7 @@
 FAMILIES = {
     "rs1b": 8, "rs1f": 8, "rs1h": 8, "sq1": 8, "ag1b": 8, "ds1": 8, "ag1f": 8, "ag1a": 8,
     "rs2b": 8, "rs2f": 8, "sq2": 8, "ag2b": 8, "ds2": 8, "ag2f": 8, "up": 4, "down": 4,
-    "hg": 4, "dy0": 4, "dy1": 16, "a": 8, "du0": 4, "du1": 4, "mirror": 3,
+    "hg": 4, "dy0": 4, "dy1": 16, "a": 16, "du0": 4, "du1": 4, "mirror": 3,
 }
 INDEX = {}
 N_SEMS = 0
@@ -336,7 +336,9 @@
             def _():
                 rs2b.start_to(r)
 
-        xdy1.append(Exchange("dy1", "dp", lambda peer, s=s: dy1.at[s], dyr.at[k, 1, s], 4 * s).start())
+        xdy1.append(Exchange("dy1", "dp", lambda peer, s=s: dy1.at[s], dyr.at[k, 1, s], 4 * s))
+        if s >= 2:
+            xdy1[-1].start()
     dyr[k, 1] = dy1[...]
     ag1f.receive()
     for s in range(slots):
@@ -353,13 +355,18 @@
 
     ag1a.receive()
 
-    def latents(peer, tick):
-        return a1a.at[:, :, pl.ds(pl.multiple_of(tick * rank + peer // 2 * 128, 128), 128)]
+    def latents(peer, tick, part=pl.ds(0, n_tensor)):
+        return a1a.at[part, :, pl.ds(pl.multiple_of(tick * rank + peer // 2 * 128, 128), 128)]
 
     xa = [
-        Exchange("a", "dp", functools.partial(latents, tick=tick), ar.at[k, tick], 4 * tick).start()
-        for tick in range(2)
+        [
+            Exchange("a", "dp", functools.partial(latents, tick=tick, part=part), ar.at[k, tick, part], 8 * i + 4 * tick).start()
+            for tick in range(2)
+        ]
+        for i, part in enumerate([pl.ds(n_tensor // 2, n_tensor // 2), pl.ds(0, n_tensor // 2)])
     ]
+    for exchange in xdy1[2:]:
+        exchange.start()
     own_a = [pltpu.make_async_copy(latents(k, tick), ar.at[k, tick], own_sem.at[1 + tick]) for tick in range(2)]
     for copy in own_a:
         copy.start()
@@ -372,7 +379,7 @@
 
     for copy in own_a:
         copy.wait()
-    for exchange in [xdy0] + xdy1 + xa:
+    for exchange in [xdy0] + xdy1[:2] + xa[0]:
         exchange.receive()
 
     @pl.when(lower)
@@ -429,6 +436,8 @@
     squares = summed(xsq2, sq2, rq2)
     a2f[t] = swish(summed(rs2f, s2f, r2f) * factor_of(unpacked(squares, half, 0)))
     ag2f = gather("ag2f", a2f).start()
+    for exchange in xdy1[2:] + xa[1]:
+        exchange.receive()
     for s in (0, 1):
         gu[s] = up_gradient(s)
         gd[s] = down_gradient(s)

time: 103 us -> 103 us (level)
  the two profiles are of different devices: /device:TPU:73 before, /device:TPU:97 now
where the time goes in v5:
time: 103 us; the launch traced here: 102 us
  Pallas kernels  102 us (99%)
    pallas_call x1, Pallas kernels, per_device(): pl.pallas_call(functools.partial(kernel, n_pipe, n_tensor, n_dp, width *...  101 us

profile of v5, /device:TPU:97, one launch (start us, length us, event | category | flops | bytes accessed | tf_op | source)
XLA Modules:
  0.0 102.5 jit_solution(3141960157359012869)
XLA Ops:
  0.6 100.8 %relay_window.1 = (bf16[1,4,32,640]{3,2,1,0:T(8,128)(2,1)S(1)}, bf16[1,4,32,640]{3,2,1,0:T(8,128)(2,1)S(1)}, f32[1,2,160,256]{3,2,1,0:T(8,128)S(1)}, f32[1,2,64,640]{3,2,1,0:T(8,128)S(1)}) custom-call(bf16[1,4,640,256]{3,2,1,0:T(8,128)(2,1)} %wd_hbm.1, bf16[1,4,256,640]{3,2,1,0:T(8,128)(2,1)} %wu_hbm.1, f32[1,4,640]{2,1,0:T(4,128)} %g_hbm.1, ...), custom_call_target="tpu_custom_call" | custom-call | tf_op jit(solution)/shard_map/relay_window/pallas_call | solution.py:495
  101.5 1.0 write_results.1
